TPU v7x, 256 devices: a whole 4x4x8 slice. The times are simulated.
256 devices in a mesh: dp: 4 (over x_hi, core), ctx: 64 (over z, y, x_lo).
Axes of the slice: x: 4 (x_hi: 2, x_lo: 2; x = x_hi * 2 + x_lo), y: 4, z: 8, core: 2. Of those that a mesh axis runs over, the one named last changes fastest.
Arguments:
- queries: bfloat16 [4, 8192, 2560], P('dp', 'ctx'), may hold values from -6 to 6
- keys: bfloat16 [4, 8192, 512], P('dp', 'ctx'), may hold values from -6 to 6
- values: bfloat16 [4, 8192, 512], P('dp', 'ctx'), may hold values from -6 to 6
- out_grad: bfloat16 [4, 8192, 2560], P('dp', 'ctx'), may hold values from -24 to 24
- layer_input: bfloat16 [4, 8192, 5120], P('dp', 'ctx'), may hold values from -16 to 16
- doc_lens: int32 [4, 16], P('dp'), may hold values from 1 to 1024, 8192 in all within a row
Outputs:
- attn_out: bfloat16 [4, 8192, 2560], P('dp', 'ctx')
- query_grad: bfloat16 [4, 8192, 2560], P('dp', 'ctx')
- key_grad: bfloat16 [4, 8192, 512], P('dp', 'ctx')
- value_grad: bfloat16 [4, 8192, 512], P('dp', 'ctx')
- weight_grad: float32 [5120, 1024], P(('dp', 'ctx'))
Inputs may be any that keep to these rules, and one draw needn't show every extreme that they name: `doc_lens`: the documents of a micro-batch lie end to end and fill its 8192 positions; in every micro-batch the longest has exactly 1024 positions.
All inputs are finite; a program needn't handle non-finite values.
Results may differ from a plain program's by a relative error of at most 0.029.
Values may be sent and summed in bfloat16 or wider, within the bound.
No kernel may reach another device: no remote copies, remote signals or barrier semaphores. Data moves between devices by JAX's collectives and lax.ppermute only.
A program may use at most 128 MiB of HBM per device.

v0:
```python
import math
import jax
import jax.numpy as jnp
from jax import lax
from jax.sharding import Mesh
from jax.sharding import PartitionSpec as P

D = 5120
HD = 128
NEGATIVE = -1e30
CTX = ("cz", "cw")


def shifted(block, distance, n_ctx):
    route = [(i - distance, i) for i in range(n_ctx) if 0 <= i - distance < n_ctx]
    return lax.ppermute(block, CTX, route)


def doc_index(lengths_row, positions):
    bounds = jnp.cumsum(lengths_row)
    return jnp.sum((positions[:, None] >= bounds[None, :]).astype(jnp.int32), axis=1)


def make_shards(n_data, n_cz, n_cw):
    n_context = n_cz * n_cw

    def shards(queries, keys, values, out_grad, layer_input, doc_lens):
        tok_rows = queries.shape[1]
        kv_width = keys.shape[2]
        heads_kv = kv_width // HD
        group = queries.shape[2] // kv_width
        inverse = 1.0 / math.sqrt(HD)
        blocks_back = min(8, n_context // 4)
        owned = D // (n_data * n_context)
        member = lax.axis_index("cw")
        chunks = layer_input[0].reshape(tok_rows, n_data, n_cz, n_cw, owned)
        chunks = chunks.transpose(3, 0, 2, 1, 4).reshape(n_cw, tok_rows, n_cz * n_data * owned)
        received = [lax.dynamic_index_in_dim(chunks, member, 0, keepdims=False)]
        for k in range(1, n_cw):
            route = [(i, (i + k) % n_cw) for i in range(n_cw)]
            outgoing = lax.dynamic_index_in_dim(chunks, (member + k) % n_cw, 0, keepdims=False)
            received.append(lax.ppermute(outgoing, "cw", route))
        column_share = jnp.concatenate(received[::-1], axis=0)
        own_pair = jnp.concatenate([keys[0], values[0]], axis=1)
        earlier = [shifted(own_pair, d, n_context) for d in range(blocks_back, 0, -1)]
        window_pair = jnp.concatenate(earlier + [own_pair], axis=0)
        span = window_pair.shape[0]
        key_win = window_pair[:, :kv_width].reshape(span, heads_kv, HD)
        value_win = window_pair[:, kv_width:].reshape(span, heads_kv, HD)
        device = lax.axis_index("cz") * n_cw + lax.axis_index("cw")
        query_pos = device * tok_rows + jnp.arange(tok_rows, dtype=jnp.int32)
        key_pos = (device - blocks_back) * tok_rows + jnp.arange(span, dtype=jnp.int32)
        query_ids = doc_index(doc_lens[0], query_pos)
        key_ids = doc_index(doc_lens[0], key_pos)
        allowed = (
            (key_pos[None, :] <= query_pos[:, None])
            & (key_ids[None, :] == query_ids[:, None])
            & (key_pos[None, :] >= 0)
        )
        query_blk = queries[0].reshape(tok_rows, heads_kv, group, HD)
        grad_blk = out_grad[0].reshape(tok_rows, heads_kv, group, HD)
        scores = (
            jnp.einsum("ighd,jgd->ghij", query_blk, key_win, preferred_element_type=jnp.float32)
            * inverse
        )
        scores = jnp.where(allowed[None, None], scores, NEGATIVE)
        peak = jnp.max(scores, axis=-1, keepdims=True)
        exponent = jnp.exp(scores - peak)
        probs = exponent / jnp.sum(exponent, axis=-1, keepdims=True)
        probs_half = probs.astype(jnp.bfloat16)
        output = jnp.einsum(
            "ghij,jgd->ighd", probs_half, value_win, preferred_element_type=jnp.float32
        )
        out_half = output.astype(jnp.bfloat16)
        delta = jnp.einsum("ighd,ighd->ghi", grad_blk, out_half, preferred_element_type=jnp.float32)
        prob_grad = jnp.einsum(
            "ighd,jgd->ghij", grad_blk, value_win, preferred_element_type=jnp.float32
        )
        score_grad = (probs * (prob_grad - delta[..., None])).astype(jnp.bfloat16)
        query_part = (
            jnp.einsum("ghij,jgd->ighd", score_grad, key_win, preferred_element_type=jnp.float32)
            * inverse
        ).astype(jnp.bfloat16)
        key_part = (
            jnp.einsum("ghij,ighd->jgd", score_grad, query_blk, preferred_element_type=jnp.float32)
            * inverse
        )
        value_part = jnp.einsum(
            "ghij,ighd->jgd", probs_half, grad_blk, preferred_element_type=jnp.float32
        )
        pair_grad = jnp.concatenate(
            [key_part.reshape(span, kv_width), value_part.reshape(span, kv_width)], axis=1
        )

        def block_back(distance):
            first_row = (blocks_back - distance) * tok_rows
            return pair_grad[first_row : first_row + tok_rows]

        total = block_back(0)
        for distance in range(1, blocks_back + 1):
            total = total + shifted(block_back(distance), -distance, n_context)
        pair_half = total.astype(jnp.bfloat16)
        grad_scale = 1.0 / math.sqrt(tok_rows * n_context * n_data)
        group_grad = lax.all_gather(pair_half, "cw", axis=0, tiled=True)
        group_grad = lax.dynamic_slice_in_dim(
            jnp.concatenate([group_grad, group_grad], axis=0),
            (member + 1) % n_cw * tok_rows,
            n_cw * tok_rows,
            0,
        )
        batch_grad = lax.dot_general(
            column_share, group_grad, (((0,), (0,)), ((), ())), preferred_element_type=jnp.float32
        )
        by_layer = lax.psum_scatter(batch_grad * grad_scale, "cz", scatter_dimension=0, tiled=True)
        weight_grad = lax.psum_scatter(by_layer, "dp", scatter_dimension=0, tiled=True)
        attn_out = out_half.reshape(tok_rows, group * kv_width)[None]
        query_grad = query_part.reshape(tok_rows, group * kv_width)[None]
        key_grad = pair_half[:, :kv_width][None]
        value_grad = pair_half[:, kv_width:][None]
        return (attn_out, query_grad, key_grad, value_grad, weight_grad)

    return shards


def solution(mesh):
    n_data = mesh.shape["dp"]
    n_context = mesh.shape["ctx"]
    n_cw = 8 if n_context % 8 == 0 else n_context
    n_cz = n_context // n_cw
    split = Mesh(mesh.devices.reshape(n_data, n_cz, n_cw), ("dp", "cz", "cw"))
    tokens = P("dp", CTX, None)
    in_specs = (tokens, tokens, tokens, tokens, tokens, P("dp", None))
    out_specs = (tokens, tokens, tokens, tokens, P(("dp", "cz", "cw"), None))
    return jax.shard_map(
        make_shards(n_data, n_cz, n_cw),
        mesh=split,
        in_specs=in_specs,
        out_specs=out_specs,
        check_vma=False,
    )
```

profile of v0, /device:TPU:14, one launch (start us, length us, event | category | flops | bytes accessed | tf_op | source)
XLA Modules:
  0.0 378.9 jit_solution(11318091829829404066)
XLA Ops:
  7.2 1.1 copy.100
  8.3 1.0 copy.101
  9.4 3.8 collective-permute-start.7
  13.1 3.2 collective-permute-start.6
  16.3 4.0 %collective-permute-start.2 = (bf16[128,1024]{0,1:T(8,128)(2,1)S(1)}, bf16[128,1024]{0,1:T(8,128)(2,1)S(1)}, u32[]{:S(2)}, u32[]{:S(2)}) collective-permute-start(bf16[128,1024]{0,1:T(8,128)(2,1)S(1)} %pad_maximum_fusion.1), channel_id=1, source_target_pairs={{0,6},{1,7},{2,8},{3,9},{4,10},{5,11},{6,12},{7,13},{8,14},{9,15},... | collective-permute-start | bytes 786440 | tf_op jit(solution)/shard_map/ppermute | solution.py:16
  20.3 3.4 collective-permute-start.1
  23.8 4.5 %collective-permute-start = (bf16[128,1024]{0,1:T(8,128)(2,1)S(1)}, bf16[128,1024]{0,1:T(8,128)(2,1)}, u32[]{:S(2)}, u32[]{:S(2)}) collective-permute-start(bf16[128,1024]{0,1:T(8,128)(2,1)S(1)} %pad_maximum_fusion.1), channel_id=1, source_target_pairs={{0,8},{1,9},{2,10},{3,11},{4,12},{5,13},{6,14},{7,15},{8,16},{9,17... | collective-permute-start | bytes 786440 | tf_op jit(solution)/shard_map/ppermute | solution.py:16
  28.3 0.7 copy.102
  29.4 1.9 and_and_fusion
  31.4 1.4 copy.107
  33.1 3.4 collective-permute-done
  36.6 3.2 collective-permute-start.3
  39.8 1.0 constant_dynamic-update-slice_fusion.8
  40.8 8.0 %collective-permute-start.4 = (bf16[128,1024]{0,1:T(8,128)(2,1)S(1)}, bf16[128,1024]{0,1:T(8,128)(2,1)S(1)}, u32[]{:S(2)}, u32[]{:S(2)}) collective-permute-start(bf16[128,1024]{0,1:T(8,128)(2,1)S(1)} %pad_maximum_fusion.1), channel_id=1, source_target_pairs={{0,4},{1,5},{2,6},{3,7},{4,8},{5,9},{6,10},{7,11},{8,12},{9,13},{1... | collective-permute-start | bytes 786440 | tf_op jit(solution)/shard_map/ppermute | solution.py:16
  48.9 8.3 %collective-permute-start.5 = (bf16[128,1024]{0,1:T(8,128)(2,1)S(1)}, bf16[128,1024]{0,1:T(8,128)(2,1)S(1)}, u32[]{:S(2)}, u32[]{:S(2)}) collective-permute-start(bf16[128,1024]{0,1:T(8,128)(2,1)S(1)} %pad_maximum_fusion.1), channel_id=1, source_target_pairs={{0,3},{1,4},{2,5},{3,6},{4,7},{5,8},{6,9},{7,10},{8,11},{9,12},{10... | collective-permute-start | bytes 786440 | tf_op jit(solution)/shard_map/ppermute | solution.py:16
  57.5 3.9 %collective-permute-done.5 = bf16[128,1024]{0,1:T(8,128)(2,1)S(1)} collective-permute-done((bf16[128,1024]{0,1:T(8,128)(2,1)S(1)}, bf16[128,1024]{0,1:T(8,128)(2,1)S(1)}, u32[]{:S(2)}, u32[]{:S(2)}) %collective-permute-start.5) | collective-permute-done | bytes 262176 | tf_op jit(solution)/shard_map/ppermute | solution.py:16
  61.7 1.3 fusion.41
  63.0 6.9 %fusion.42 = (f32[4,5,128]{2,1,0:T(8,128)S(1)}, f32[4,5,128,1152]{2,3,1,0:T(8,128)}) fusion(pred[128,1152]{0,1:T(8,128)(4,1)S(1)} %copy-done.11, bf16[1152,4,128,1]{0,2,3,1:T(8,128)(2,1)S(1)} %bitcast.102, bf16[128,4,5,128]{0,3,2,1:T(8,128)(2,1)S(1)} %bitcast.105), kind=kOutput, calls=%fused_computation.99 | convolution fusion | flops 766772352 | bytes 13789184 | tf_op jit(solution)/shard_map/sub | solution.py:68
  69.9 5.9 %fusion.8 = bf16[4,5,128,1152]{2,3,1,0:T(8,128)(2,1)S(1)} fusion(f32[4,5,128,1152]{2,3,1,0:T(8,128)} %get-tuple-element.51, f32[4,5,128]{2,1,0:T(8,128)S(1)} %get-tuple-element.50), kind=kLoop, calls=%fused_computation.27 | loop fusion | flops 5898240 | bytes 17704960 | tf_op jit(solution)/shard_map/convert_element_type | solution.py:70
  75.8 3.3 fusion.43
  79.0 2.0 copy.114
  81.1 5.2 %fusion.19 = (f32[4,5,128]{2,1,0:T(8,128)S(1)}, bf16[4,128,5,128]{3,1,2,0:T(8,128)(2,1)}) fusion(bf16[4,5,128,128]{2,3,1,0:T(8,128)(2,1)S(1)} %bitcast.98, bf16[1152,4,128,1]{0,2,3,1:T(8,128)(2,1)} %bitcast.100, bf16[4,5,128,1152]{2,3,1,0:T(8,128)(2,1)} %copy-done), kind=kOutput, calls=%fused_computation.40 | convolution fusion | flops 756610560 | bytes 8398848 | tf_op jit(solution)/shard_map/ghij,jgd->ighd/dot_general | solution.py:71
  86.3 5.6 %fusion.3 = bf16[4,5,128,1152]{2,3,1,0:T(8,128)(2,1)S(1)} fusion(bf16[1152,4,128,1]{0,2,3,1:T(8,128)(2,1)S(1)} %bitcast.101, bf16[128,4,5,128]{0,3,2,1:T(8,128)(2,1)S(1)} %bitcast.99, f32[4,5,128]{2,1,0:T(8,128)S(1)} %get-tuple-element.52, f32[4,5,128,1152]{2,3,1,0:T(8,128)} %get-tuple-element.51, f32[4,5,128]{2,1,0:T(8,128)S(1)} %get-tuple-element.50), kind=kOutput, calls=%fused_computation.3 | convolution fusion | flops 766771200 | bytes 19550208 | tf_op jit(solution)/shard_map/ighd,jgd->ghij/dot_general | solution.py:76
  91.9 3.3 fusion.9
  95.2 3.1 copy.113
  98.3 2.0 fusion.30
  100.3 3.7 collective-permute-start.8
  104.1 1.9 collective-permute-start.9
  106.0 2.1 collective-permute-start.10
  108.1 1.3 collective-permute-start.11
  109.4 1.3 collective-permute-start.12
  110.7 7.2 %collective-permute-done.8 = f32[128,1024]{1,0:T(8,128)S(1)} collective-permute-done((f32[128,1024]{1,0:T(8,128)S(1)}, f32[128,1024]{1,0:T(8,128)S(1)}, u32[]{:S(2)}, u32[]{:S(2)}) %collective-permute-start.8) | collective-permute-done | bytes 524320 | tf_op jit(solution)/shard_map/ppermute | solution.py:16
  118.0 1.3 collective-permute-start.13
  119.3 17.8 %collective-permute-done.9 = f32[128,1024]{1,0:T(8,128)S(1)} collective-permute-done((f32[128,1024]{1,0:T(8,128)S(1)}, f32[128,1024]{1,0:T(8,128)S(1)}, u32[]{:S(2)}, u32[]{:S(2)}) %collective-permute-start.9) | collective-permute-done | bytes 524320 | tf_op jit(solution)/shard_map/ppermute | solution.py:16
  137.0 1.3 collective-permute-start.15
  138.3 1.3 collective-permute-start.14
  139.6 14.1 %collective-permute-done.11 = f32[128,1024]{1,0:T(8,128)S(1)} collective-permute-done((f32[128,1024]{1,0:T(8,128)S(1)}, f32[128,1024]{1,0:T(8,128)S(1)}, u32[]{:S(2)}, u32[]{:S(2)}) %collective-permute-start.11) | collective-permute-done | bytes 524320 | tf_op jit(solution)/shard_map/ppermute | solution.py:16
  153.8 30.6 %collective-permute-done.12 = f32[128,1024]{1,0:T(8,128)S(1)} collective-permute-done((f32[128,1024]{1,0:T(8,128)S(1)}, f32[128,1024]{1,0:T(8,128)S(1)}, u32[]{:S(2)}, u32[]{:S(2)}) %collective-permute-start.12) | collective-permute-done | bytes 524320 | tf_op jit(solution)/shard_map/ppermute | solution.py:16
  184.3 31.7 %collective-permute-done.13 = f32[128,1024]{1,0:T(8,128)S(1)} collective-permute-done((f32[128,1024]{1,0:T(8,128)S(1)}, f32[128,1024]{1,0:T(8,128)S(1)}, u32[]{:S(2)}, u32[]{:S(2)}) %collective-permute-start.13) | collective-permute-done | bytes 524320 | tf_op jit(solution)/shard_map/ppermute | solution.py:16
  216.1 1.1 fusion.36
  217.4 1.8 copy.115
  219.7 3.6 constant_dynamic-slice_fusion.1
  223.3 1.8 copy.117
  225.1 22.3 %collective-permute-start.16 = (bf16[128,640]{1,0:T(8,128)(2,1)}, bf16[128,640]{1,0:T(8,128)(2,1)S(1)}, u32[]{:S(2)}, u32[]{:S(2)}) collective-permute-start(bf16[128,640]{1,0:T(8,128)(2,1)} %bitcast.36), channel_id=1, source_target_pairs={{0,7},{1,0},{2,1},{3,2},{4,3},{5,4},{6,5},{7,6},{8,15},{9,8},{10,9... | collective-permute-start | bytes 491528 | tf_op jit(solution)/shard_map/ppermute | solution.py:42
  247.3 1.8 copy.118
  249.6 3.0 collective-permute-start.19
  252.7 1.6 collective-permute-start.20
  254.9 2.1 collective-permute-start.21
  257.0 0.7 constant_dynamic-update-slice_fusion.15
  257.7 5.9 %collective-permute-done.17 = bf16[128,640]{1,0:T(8,128)(2,1)S(1)} collective-permute-done((bf16[128,640]{1,0:T(8,128)(2,1)}, bf16[128,640]{1,0:T(8,128)(2,1)S(1)}, u32[]{:S(2)}, u32[]{:S(2)}) %collective-permute-start.17) | collective-permute-done | bytes 163872 | tf_op jit(solution)/shard_map/ppermute | solution.py:42
  263.6 0.7 constant_dynamic-update-slice_fusion.14
  265.7 4.3 %collective-permute-done.20 = bf16[128,640]{1,0:T(8,128)(2,1)S(1)} collective-permute-done((bf16[128,640]{1,0:T(8,128)(2,1)S(1)}, bf16[128,640]{1,0:T(8,128)(2,1)S(1)}, u32[]{:S(2)}, u32[]{:S(2)}) %collective-permute-start.20) | collective-permute-done | bytes 163872 | tf_op jit(solution)/shard_map/ppermute | solution.py:42
  270.6 0.7 constant_dynamic-update-slice_fusion.10
  271.3 1.9 collective-permute-done.22
  274.5 25.8 %all-gather.2.cloned.1.call-done = bf16[1024,1024]{1,0:T(8,128)(2,1)} async-done(((bf16[128,1024]{1,0:T(8,128)(2,1)}), bf16[1024,1024]{1,0:T(8,128)(2,1)}) %all-gather.2.cloned.1.call-update) | async-done | bytes 2097168 | tf_op jit(solution)/shard_map/all_gather | solution.py:104
  300.3 5.1 %fusion.15 = f32[640,1024]{1,0:T(8,128)} fusion(bf16[1024,640]{1,0:T(8,128)(2,1)} %bitcast_dynamic-update-slice_fusion, s32[]{:T(128)S(6)} %select_n.81, bf16[1024,1024]{1,0:T(8,128)(2,1)} %all-gather.2.cloned.1.call-done), kind=kOutput, calls=%fused_computation.35 | convolution fusion | flops 1347026944 | bytes 6029316 | tf_op jit(solution)/shard_map/dot_general | solution.py:111
  307.4 3.9 %fusion.18 = bf16[4,128,5,128]{3,1,2,0:T(8,128)(2,1)S(1)} fusion(bf16[1152,4,128,1]{0,2,3,1:T(8,128)(2,1)S(1)} %bitcast.103, bf16[4,5,128,1152]{2,3,1,0:T(8,128)(2,1)} %copy-done.1), kind=kOutput, calls=%fused_computation.37 | convolution fusion | flops 755630080 | bytes 7733248 | tf_op jit(solution)/shard_map/ghij,jgd->ighd/dot_general | solution.py:81
  311.3 1.1 copy.126
  312.4 1.1 copy.125
  313.5 38.7 %reduce-scatter.4.cloned.1.call-done = f32[80,1024]{1,0:T(8,128)} async-done(((f32[640,1024]{1,0:T(8,128)}), f32[80,1024]{1,0:T(8,128)}) %reduce-scatter.4.cloned.1.call-update) | async-done | bytes 327696 | tf_op jit(solution)/shard_map/reduce_scatter | solution.py:114
  352.2 11.9 %fusion = f32[24,1024]{1,0:T(8,128)S(1)} fusion(f32[80,1024]{1,0:T(8,128)} %reduce-scatter.4.cloned.1.call-done), kind=kCustom, calls=%all-reduce-scatter | all-reduce-scatter fusion | flops 98305 | bytes 427008
  364.2 1.9 collective-permute-start.23
  366.1 0.7 slice_bitcast_fusion
  366.8 4.4 %collective-permute-done.23 = f32[12,1024]{1,0:T(8,128)S(1)} collective-permute-done((f32[12,1024]{1,0:T(8,128)S(1)}, f32[12,1024]{1,0:T(8,128)S(1)}, u32[]{:S(2)}, u32[]{:S(2)}) %collective-permute-start.23) | collective-permute-done | bytes 49184
  (80 shorter events, 8.5 us)
Async XLA Ops:
  7.2 25.6 %copy-start.10 = (bf16[1,128,2560]{2,1,0:T(8,128)(2,1)S(1)}, bf16[1,128,2560]{2,1,0:T(8,128)(2,1)}, u32[]{:S(2)}) copy-start(bf16[1,128,2560]{2,1,0:T(8,128)(2,1)} %param.6) | copy-start | bytes 1966084
  7.2 293.1 %all-gather.2.cloned.1.call-start = ((), (), s32[]{:S(2)}) async-start(), calls=%async_computation.1 | async-start | bytes 2359296 | tf_op jit(solution)/shard_map/all_gather | solution.py:104
  9.4 52.2 %collective-permute-start.7 = (bf16[128,1024]{0,1:T(8,128)(2,1)S(1)}, bf16[128,1024]{0,1:T(8,128)(2,1)S(1)}, u32[]{:S(2)}, u32[]{:S(2)}) collective-permute-start(bf16[128,1024]{0,1:T(8,128)(2,1)S(1)} %pad_maximum_fusion.1), channel_id=1, source_target_pairs={{0,1},{1,2},{2,3},{3,4},{4,5},{5,6},{6,7},{7,8},{8,9},{9,10},{10,1... | collective-permute-start | bytes 786440 | tf_op jit(solution)/shard_map/ppermute | solution.py:16
  13.1 48.4 %collective-permute-start.6 = (bf16[128,1024]{0,1:T(8,128)(2,1)S(1)}, bf16[128,1024]{0,1:T(8,128)(2,1)S(1)}, u32[]{:S(2)}, u32[]{:S(2)}) collective-permute-start(bf16[128,1024]{0,1:T(8,128)(2,1)S(1)} %pad_maximum_fusion.1), channel_id=1, source_target_pairs={{0,2},{1,3},{2,4},{3,5},{4,6},{5,7},{6,8},{7,9},{8,10},{9,11},{10,... | collective-permute-start | bytes 786440 | tf_op jit(solution)/shard_map/ppermute | solution.py:16
  16.3 32.6 %collective-permute-start.2 = (bf16[128,1024]{0,1:T(8,128)(2,1)S(1)}, bf16[128,1024]{0,1:T(8,128)(2,1)S(1)}, u32[]{:S(2)}, u32[]{:S(2)}) collective-permute-start(bf16[128,1024]{0,1:T(8,128)(2,1)S(1)} %pad_maximum_fusion.1), channel_id=1, source_target_pairs={{0,6},{1,7},{2,8},{3,9},{4,10},{5,11},{6,12},{7,13},{8,14},{9,15},... | collective-permute-start | bytes 786440 | tf_op jit(solution)/shard_map/ppermute | solution.py:16
  20.3 20.4 %collective-permute-start.1 = (bf16[128,1024]{0,1:T(8,128)(2,1)S(1)}, bf16[128,1024]{0,1:T(8,128)(2,1)S(1)}, u32[]{:S(2)}, u32[]{:S(2)}) collective-permute-start(bf16[128,1024]{0,1:T(8,128)(2,1)S(1)} %pad_maximum_fusion.1), channel_id=1, source_target_pairs={{0,7},{1,8},{2,9},{3,10},{4,11},{5,12},{6,13},{7,14},{8,15},{9,16}... | collective-permute-start | bytes 786440 | tf_op jit(solution)/shard_map/ppermute | solution.py:16
  23.8 12.8 %collective-permute-start = (bf16[128,1024]{0,1:T(8,128)(2,1)S(1)}, bf16[128,1024]{0,1:T(8,128)(2,1)}, u32[]{:S(2)}, u32[]{:S(2)}) collective-permute-start(bf16[128,1024]{0,1:T(8,128)(2,1)S(1)} %pad_maximum_fusion.1), channel_id=1, source_target_pairs={{0,8},{1,9},{2,10},{3,11},{4,12},{5,13},{6,14},{7,15},{8,16},{9,17... | collective-permute-start | bytes 786440 | tf_op jit(solution)/shard_map/ppermute | solution.py:16
  33.1 29.9 %copy-start.7 = (bf16[1,128,2560]{1,2,0:T(8,128)(2,1)}, bf16[1,128,2560]{1,2,0:T(8,128)(2,1)S(1)}, u32[]{:S(2)}) copy-start(bf16[1,128,2560]{1,2,0:T(8,128)(2,1)S(1)} %copy.103) | copy-start | bytes 1966084
  36.6 20.8 %collective-permute-start.3 = (bf16[128,1024]{0,1:T(8,128)(2,1)S(1)}, bf16[128,1024]{0,1:T(8,128)(2,1)S(1)}, u32[]{:S(2)}, u32[]{:S(2)}) collective-permute-start(bf16[128,1024]{0,1:T(8,128)(2,1)S(1)} %pad_maximum_fusion.1), channel_id=1, source_target_pairs={{0,5},{1,6},{2,7},{3,8},{4,9},{5,10},{6,11},{7,12},{8,13},{9,14},{... | collective-permute-start | bytes 786440 | tf_op jit(solution)/shard_map/ppermute | solution.py:16
  40.8 16.6 %collective-permute-start.4 = (bf16[128,1024]{0,1:T(8,128)(2,1)S(1)}, bf16[128,1024]{0,1:T(8,128)(2,1)S(1)}, u32[]{:S(2)}, u32[]{:S(2)}) collective-permute-start(bf16[128,1024]{0,1:T(8,128)(2,1)S(1)} %pad_maximum_fusion.1), channel_id=1, source_target_pairs={{0,4},{1,5},{2,6},{3,7},{4,8},{5,9},{6,10},{7,11},{8,12},{9,13},{1... | collective-permute-start | bytes 786440 | tf_op jit(solution)/shard_map/ppermute | solution.py:16
  48.9 12.5 %collective-permute-start.5 = (bf16[128,1024]{0,1:T(8,128)(2,1)S(1)}, bf16[128,1024]{0,1:T(8,128)(2,1)S(1)}, u32[]{:S(2)}, u32[]{:S(2)}) collective-permute-start(bf16[128,1024]{0,1:T(8,128)(2,1)S(1)} %pad_maximum_fusion.1), channel_id=1, source_target_pairs={{0,3},{1,4},{2,5},{3,6},{4,7},{5,8},{6,9},{7,10},{8,11},{9,12},{10... | collective-permute-start | bytes 786440 | tf_op jit(solution)/shard_map/ppermute | solution.py:16
  61.7 1.3 copy-start.11
  63.0 6.9 %copy-start.4 = (bf16[1152,512]{0,1:T(8,128)(2,1)}, bf16[1152,512]{0,1:T(8,128)(2,1)S(1)}, u32[]{:S(2)}) copy-start(bf16[1152,512]{0,1:T(8,128)(2,1)S(1)} %get-tuple-element.38) | copy-start | bytes 3538948
  75.8 3.3 copy-start
  81.1 5.2 %copy-start.3 = (bf16[1152,512]{0,1:T(8,128)(2,1)S(1)}, bf16[1152,512]{0,1:T(8,128)(2,1)}, u32[]{:S(2)}) copy-start(bf16[1152,512]{0,1:T(8,128)(2,1)} %get-tuple-element.39) | copy-start | bytes 3538948
  86.3 5.6 %copy-start.8 = (bf16[1,128,2560]{1,2,0:T(8,128)(2,1)S(1)}, bf16[1,128,2560]{1,2,0:T(8,128)(2,1)}, u32[]{:S(2)}) copy-start(bf16[1,128,2560]{1,2,0:T(8,128)(2,1)} %copy-done.7) | copy-start | bytes 1966084
  91.9 3.3 copy-start.1
  98.3 117.8 %copy-start.2 = (f32[1152,512]{1,0:T(8,128)S(1)}, f32[1152,512]{1,0:T(8,128)}, u32[]{:S(2)}) copy-start(f32[1152,512]{1,0:T(8,128)} %copy.113) | copy-start | bytes 7077892
  100.3 17.6 %collective-permute-start.8 = (f32[128,1024]{1,0:T(8,128)S(1)}, f32[128,1024]{1,0:T(8,128)S(1)}, u32[]{:S(2)}, u32[]{:S(2)}) collective-permute-start(f32[128,1024]{1,0:T(8,128)S(1)} %get-tuple-element.30), channel_id=1, source_target_pairs={{1,0},{2,1},{3,2},{4,3},{5,4},{6,5},{7,6},{8,7},{9,8},{10,9},{11,1... | collective-permute-start | bytes 1572872 | tf_op jit(solution)/shard_map/ppermute | solution.py:16
  104.1 33.0 %collective-permute-start.9 = (f32[128,1024]{1,0:T(8,128)S(1)}, f32[128,1024]{1,0:T(8,128)S(1)}, u32[]{:S(2)}, u32[]{:S(2)}) collective-permute-start(f32[128,1024]{1,0:T(8,128)S(1)} %get-tuple-element.31), channel_id=1, source_target_pairs={{2,0},{3,1},{4,2},{5,3},{6,4},{7,5},{8,6},{9,7},{10,8},{11,9},{12,... | collective-permute-start | bytes 1572872 | tf_op jit(solution)/shard_map/ppermute | solution.py:16
  106.0 32.3 %collective-permute-start.10 = (f32[128,1024]{1,0:T(8,128)S(1)}, f32[128,1024]{1,0:T(8,128)S(1)}, u32[]{:S(2)}, u32[]{:S(2)}) collective-permute-start(f32[128,1024]{1,0:T(8,128)S(1)} %get-tuple-element.32), channel_id=1, source_target_pairs={{3,0},{4,1},{5,2},{6,3},{7,4},{8,5},{9,6},{10,7},{11,8},{12,9},{13... | collective-permute-start | bytes 1572872 | tf_op jit(solution)/shard_map/ppermute | solution.py:16
  108.1 45.6 %collective-permute-start.11 = (f32[128,1024]{1,0:T(8,128)S(1)}, f32[128,1024]{1,0:T(8,128)S(1)}, u32[]{:S(2)}, u32[]{:S(2)}) collective-permute-start(f32[128,1024]{1,0:T(8,128)S(1)} %get-tuple-element.33), channel_id=1, source_target_pairs={{4,0},{5,1},{6,2},{7,3},{8,4},{9,5},{10,6},{11,7},{12,8},{13,9},{1... | collective-permute-start | bytes 1572872 | tf_op jit(solution)/shard_map/ppermute | solution.py:16
  109.4 74.9 %collective-permute-start.12 = (f32[128,1024]{1,0:T(8,128)S(1)}, f32[128,1024]{1,0:T(8,128)S(1)}, u32[]{:S(2)}, u32[]{:S(2)}) collective-permute-start(f32[128,1024]{1,0:T(8,128)S(1)} %get-tuple-element.34), channel_id=1, source_target_pairs={{5,0},{6,1},{7,2},{8,3},{9,4},{10,5},{11,6},{12,7},{13,8},{14,9},{... | collective-permute-start | bytes 1572872 | tf_op jit(solution)/shard_map/ppermute | solution.py:16
  118.0 98.1 %collective-permute-start.13 = (f32[128,1024]{1,0:T(8,128)S(1)}, f32[128,1024]{1,0:T(8,128)S(1)}, u32[]{:S(2)}, u32[]{:S(2)}) collective-permute-start(f32[128,1024]{1,0:T(8,128)S(1)} %get-tuple-element.35), channel_id=1, source_target_pairs={{6,0},{7,1},{8,2},{9,3},{10,4},{11,5},{12,6},{13,7},{14,8},{15,9},... | collective-permute-start | bytes 1572872 | tf_op jit(solution)/shard_map/ppermute | solution.py:16
  137.0 79.0 %collective-permute-start.15 = (f32[128,1024]{1,0:T(8,128)S(1)}, f32[128,1024]{1,0:T(8,128)S(1)}, u32[]{:S(2)}, u32[]{:S(2)}) collective-permute-start(f32[128,1024]{1,0:T(8,128)S(1)} %get-tuple-element.36), channel_id=1, source_target_pairs={{8,0},{9,1},{10,2},{11,3},{12,4},{13,5},{14,6},{15,7},{16,8},{17,9... | collective-permute-start | bytes 1572872 | tf_op jit(solution)/shard_map/ppermute | solution.py:16
  138.3 77.7 %collective-permute-start.14 = (f32[128,1024]{1,0:T(8,128)S(1)}, f32[128,1024]{1,0:T(8,128)S(1)}, u32[]{:S(2)}, u32[]{:S(2)}) collective-permute-start(f32[128,1024]{1,0:T(8,128)S(1)} %get-tuple-element.37), channel_id=1, source_target_pairs={{7,0},{8,1},{9,2},{10,3},{11,4},{12,5},{13,6},{14,7},{15,8},{16,9}... | collective-permute-start | bytes 1572872 | tf_op jit(solution)/shard_map/ppermute | solution.py:16
  217.2 135.0 %reduce-scatter.4.cloned.1.call-start = ((), (), s32[]{:S(2)}) async-start(), calls=%async_computation.2 | async-start | bytes 2949120 | tf_op jit(solution)/shard_map/reduce_scatter | solution.py:114
  225.1 29.8 %collective-permute-start.16 = (bf16[128,640]{1,0:T(8,128)(2,1)}, bf16[128,640]{1,0:T(8,128)(2,1)S(1)}, u32[]{:S(2)}, u32[]{:S(2)}) collective-permute-start(bf16[128,640]{1,0:T(8,128)(2,1)} %bitcast.36), channel_id=1, source_target_pairs={{0,7},{1,0},{2,1},{3,2},{4,3},{5,4},{6,5},{7,6},{8,15},{9,8},{10,9... | collective-permute-start | bytes 491528 | tf_op jit(solution)/shard_map/ppermute | solution.py:42
  249.1 14.5 %collective-permute-start.17 = (bf16[128,640]{1,0:T(8,128)(2,1)}, bf16[128,640]{1,0:T(8,128)(2,1)S(1)}, u32[]{:S(2)}, u32[]{:S(2)}) collective-permute-start(bf16[128,640]{1,0:T(8,128)(2,1)} %bitcast.37), channel_id=1, source_target_pairs={{0,6},{1,7},{2,0},{3,1},{4,2},{5,3},{6,4},{7,5},{8,14},{9,15},{10,... | collective-permute-start | bytes 491528 | tf_op jit(solution)/shard_map/ppermute | solution.py:42
  249.3 15.0 %collective-permute-start.18 = (bf16[128,640]{1,0:T(8,128)(2,1)S(1)}, bf16[128,640]{1,0:T(8,128)(2,1)S(1)}, u32[]{:S(2)}, u32[]{:S(2)}) collective-permute-start(bf16[128,640]{1,0:T(8,128)(2,1)S(1)} %bitcast.115), channel_id=1, source_target_pairs={{0,5},{1,6},{2,7},{3,0},{4,1},{5,2},{6,3},{7,4},{8,13},{9,14},{10,... | collective-permute-start | bytes 491528 | tf_op jit(solution)/shard_map/ppermute | solution.py:42
  249.6 15.4 %collective-permute-start.19 = (bf16[128,640]{1,0:T(8,128)(2,1)S(1)}, bf16[128,640]{1,0:T(8,128)(2,1)S(1)}, u32[]{:S(2)}, u32[]{:S(2)}) collective-permute-start(bf16[128,640]{1,0:T(8,128)(2,1)S(1)} %bitcast.113), channel_id=1, source_target_pairs={{0,4},{1,5},{2,6},{3,7},{4,0},{5,1},{6,2},{7,3},{8,12},{9,13},{10,... | collective-permute-start | bytes 491528 | tf_op jit(solution)/shard_map/ppermute | solution.py:42
  252.7 17.2 %collective-permute-start.20 = (bf16[128,640]{1,0:T(8,128)(2,1)S(1)}, bf16[128,640]{1,0:T(8,128)(2,1)S(1)}, u32[]{:S(2)}, u32[]{:S(2)}) collective-permute-start(bf16[128,640]{1,0:T(8,128)(2,1)S(1)} %bitcast.112), channel_id=1, source_target_pairs={{0,3},{1,4},{2,5},{3,6},{4,7},{5,0},{6,1},{7,2},{8,11},{9,12},{10,... | collective-permute-start | bytes 491528 | tf_op jit(solution)/shard_map/ppermute | solution.py:42
  254.9 15.7 %collective-permute-start.21 = (bf16[128,640]{1,0:T(8,128)(2,1)S(1)}, bf16[128,640]{1,0:T(8,128)(2,1)S(1)}, u32[]{:S(2)}, u32[]{:S(2)}) collective-permute-start(bf16[128,640]{1,0:T(8,128)(2,1)S(1)} %bitcast.116), channel_id=1, source_target_pairs={{0,2},{1,3},{2,4},{3,5},{4,6},{5,7},{6,0},{7,1},{8,10},{9,11},{10,... | collective-permute-start | bytes 491528 | tf_op jit(solution)/shard_map/ppermute | solution.py:42
  263.6 9.6 %collective-permute-start.22 = (bf16[128,640]{1,0:T(8,128)(2,1)S(1)}, bf16[128,640]{1,0:T(8,128)(2,1)S(1)}, u32[]{:S(2)}, u32[]{:S(2)}) collective-permute-start(bf16[128,640]{1,0:T(8,128)(2,1)S(1)} %bitcast.114), channel_id=1, source_target_pairs={{0,1},{1,2},{2,3},{3,4},{4,5},{5,6},{6,7},{7,0},{8,9},{9,10},{10,1... | collective-permute-start | bytes 491528 | tf_op jit(solution)/shard_map/ppermute | solution.py:42
  305.4 0.7 copy-start.12
  305.4 1.9 copy-start.5
  307.4 5.1 %copy-start.6 = (bf16[4,128,5,128]{3,1,2,0:T(8,128)(2,1)S(1)}, bf16[4,128,5,128]{3,1,2,0:T(8,128)(2,1)}, u32[]{:S(2)}) copy-start(bf16[4,128,5,128]{3,1,2,0:T(8,128)(2,1)} %get-tuple-element.53) | copy-start | bytes 1966084
  311.3 54.8 %copy-start.9 = (bf16[128,1024]{1,0:T(8,128)(2,1)S(1)}, bf16[128,1024]{1,0:T(8,128)(2,1)}, u32[]{:S(2)}) copy-start(bf16[128,1024]{1,0:T(8,128)(2,1)} %fusion.36) | copy-start | bytes 786436
  364.2 7.1 %collective-permute-start.23 = (f32[12,1024]{1,0:T(8,128)S(1)}, f32[12,1024]{1,0:T(8,128)S(1)}, u32[]{:S(2)}, u32[]{:S(2)}) collective-permute-start(f32[12,1024]{1,0:T(8,128)S(1)} %slice.72), channel_id=1, source_target_pairs={{0,64},{64,128},{128,192},{1,65},{65,129},{129,193},{2,66},{66,130... | collective-permute-start | bytes 147464
Sparse Core Ops, SparseCore 0:
  217.4 82.9 all-gather.1
  305.6 46.6 reduce-scatter.3
where the time goes:
time: 380 us; the launch traced here: 379 us
  waiting for transfers between devices  190 us (50%)
  starting transfers between devices  83.7 us (22%)
  local copies, waits for them, and re-layouts  33.4 us (9%)
  matrix products  33.2 us (9%)
  between operations  15.4 us (4%)
  blocking collectives  11.9 us (3%)
  other arithmetic  11.4 us (3%)
    ppermute x16, waiting for transfers between devices, shifted(): return lax.ppermute(block, CTX, route)  109 us
    ppermute x16, starting transfers between devices, shifted(): return lax.ppermute(block, CTX, route)  52.7 us
    reduce_scatter x1, waiting for transfers between devices, shards(): lax.psum_scatter(batch_grad * grad_scale, 'cz', scatter_dimension=0, tile...  38.7 us
    ppermute x7, starting transfers between devices, shards(): received.append(lax.ppermute(outgoing, 'cw', route))  29 us
    all_gather x1, waiting for transfers between devices, shards(): group_grad = lax.all_gather(pair_half, 'cw', axis=0, tiled=True)  25.8 us
    unnamed x52, local copies, waits for them, and re-layouts  16.1 us
    ppermute x7, waiting for transfers between devices, shards(): received.append(lax.ppermute(outgoing, 'cw', route))  12.1 us
    unnamed x1, blocking collectives  11.9 us
  transfers between devices with their start and end apart: 26, of which 13 were waited for; matrix products, arithmetic and copies ran while one was open for 8% of the time, Pallas kernels for 0%

commit v1 on v0

--- a/solution.py
+++ b/solution.py
@@ -1,3 +1,4 @@
+import functools
 import math
 import jax
 import jax.numpy as jnp
@@ -9,6 +10,17 @@
 HD = 128
 NEGATIVE = -1e30
 CTX = ("cz", "cw")
+
+
+def bind_the_trails(body, device_axis):
+    front = lax.axis_size(device_axis)
+    finding = jnp.stack([body] * front, axis=0)
+    r2 = lax.all_to_all(finding, device_axis, 0, 0)
+    back = jnp.concatenate(r2, axis=0)
+    return back
+
+
+wrap_view = functools.partial(bind_the_trails, device_axis="cw")
 
 
 def shifted(block, distance, n_ctx):
@@ -101,7 +113,7 @@
             total = total + shifted(block_back(distance), -distance, n_context)
         pair_half = total.astype(jnp.bfloat16)
         grad_scale = 1.0 / math.sqrt(tok_rows * n_context * n_data)
-        group_grad = lax.all_gather(pair_half, "cw", axis=0, tiled=True)
+        group_grad = wrap_view(pair_half)
         group_grad = lax.dynamic_slice_in_dim(
             jnp.concatenate([group_grad, group_grad], axis=0),
             (member + 1) % n_cw * tok_rows,

time: 380 us -> 364 us (0.958)
  waiting for transfers between devices: 190 us -> 166 us
  starting transfers between devices: 83.7 us -> 91.7 us
    all_gather x1 -> x0, waiting for transfers between devices: 25.8 us -> none  [shards(): group_grad = lax.all_gather(pair_half, 'cw', axis=0, tiled=True)]
    all_to_all x0 -> x1, starting transfers between devices: none -> 25 us  [bind_the_trails(): r2 = lax.all_to_all(finding, device_axis, 0, 0)]
    ppermute x7, starting transfers between devices: 29 us -> 12 us  [shards(): received.append(lax.ppermute(outgoing, 'cw', route))]
  transfers between devices with their start and end apart: 26 -> 26, of which waited for: 13 -> 11; matrix products, arithmetic and copies ran while one was open for 8% -> 8% of each run, Pallas kernels for 0% -> 0%
where the time goes in v1:
time: 364 us; the launch traced here: 363 us
  waiting for transfers between devices  166 us (46%)
  starting transfers between devices  91.7 us (25%)
  local copies, waits for them, and re-layouts  34.2 us (9%)
  matrix products  33.3 us (9%)
  between operations  15.2 us (4%)
  blocking collectives  11.5 us (3%)
  other arithmetic  10.8 us (3%)
    ppermute x16, waiting for transfers between devices, shifted(): return lax.ppermute(block, CTX, route)  109 us
    ppermute x16, starting transfers between devices, shifted(): return lax.ppermute(block, CTX, route)  52.7 us
    reduce_scatter x1, waiting for transfers between devices, shards(): lax.psum_scatter(batch_grad * grad_scale, 'cz', scatter_dimension=0, tile...  39.6 us
    all_to_all x1, starting transfers between devices, bind_the_trails(): r2 = lax.all_to_all(finding, device_axis, 0, 0)  25 us
    unnamed x52, local copies, waits for them, and re-layouts  15.1 us
    ppermute x7, waiting for transfers between devices, shards(): received.append(lax.ppermute(outgoing, 'cw', route))  13.6 us
    ppermute x7, starting transfers between devices, shards(): received.append(lax.ppermute(outgoing, 'cw', route))  12 us
    unnamed x1, blocking collectives  11.5 us
  transfers between devices with their start and end apart: 26, of which 11 were waited for; matrix products, arithmetic and copies ran while one was open for 8% of the time, Pallas kernels for 0%

profile of v1, /device:TPU:14, one launch (start us, length us, event | category | flops | bytes accessed | tf_op | source)
XLA Modules:
  0.0 363.1 jit_solution(13543950536707353296)
XLA Ops:
  7.2 1.1 copy.100
  8.3 1.0 copy.101
  9.3 3.8 %collective-permute-start.7 = (bf16[128,1024]{0,1:T(8,128)(2,1)S(1)}, bf16[128,1024]{0,1:T(8,128)(2,1)S(1)}, u32[]{:S(2)}, u32[]{:S(2)}) collective-permute-start(bf16[128,1024]{0,1:T(8,128)(2,1)S(1)} %pad_maximum_fusion.1), channel_id=1, source_target_pairs={{0,1},{1,2},{2,3},{3,4},{4,5},{5,6},{6,7},{7,8},{8,9},{9,10},{10,1... | collective-permute-start | bytes 786440 | tf_op jit(solution)/shard_map/ppermute | solution.py:28
  13.1 3.2 collective-permute-start.6
  16.3 4.0 %collective-permute-start.2 = (bf16[128,1024]{0,1:T(8,128)(2,1)S(1)}, bf16[128,1024]{0,1:T(8,128)(2,1)S(1)}, u32[]{:S(2)}, u32[]{:S(2)}) collective-permute-start(bf16[128,1024]{0,1:T(8,128)(2,1)S(1)} %pad_maximum_fusion.1), channel_id=1, source_target_pairs={{0,6},{1,7},{2,8},{3,9},{4,10},{5,11},{6,12},{7,13},{8,14},{9,15},... | collective-permute-start | bytes 786440 | tf_op jit(solution)/shard_map/ppermute | solution.py:28
  20.3 3.4 collective-permute-start.1
  23.8 4.5 %collective-permute-start = (bf16[128,1024]{0,1:T(8,128)(2,1)S(1)}, bf16[128,1024]{0,1:T(8,128)(2,1)}, u32[]{:S(2)}, u32[]{:S(2)}) collective-permute-start(bf16[128,1024]{0,1:T(8,128)(2,1)S(1)} %pad_maximum_fusion.1), channel_id=1, source_target_pairs={{0,8},{1,9},{2,10},{3,11},{4,12},{5,13},{6,14},{7,15},{8,16},{9,17... | collective-permute-start | bytes 786440 | tf_op jit(solution)/shard_map/ppermute | solution.py:28
  28.3 0.7 copy.102
  29.4 1.9 and_and_fusion
  31.3 1.4 copy.107
  33.1 3.4 collective-permute-done
  36.5 3.2 collective-permute-start.3
  39.7 1.0 constant_dynamic-update-slice_fusion.8
  40.7 8.0 %collective-permute-start.4 = (bf16[128,1024]{0,1:T(8,128)(2,1)S(1)}, bf16[128,1024]{0,1:T(8,128)(2,1)S(1)}, u32[]{:S(2)}, u32[]{:S(2)}) collective-permute-start(bf16[128,1024]{0,1:T(8,128)(2,1)S(1)} %pad_maximum_fusion.1), channel_id=1, source_target_pairs={{0,4},{1,5},{2,6},{3,7},{4,8},{5,9},{6,10},{7,11},{8,12},{9,13},{1... | collective-permute-start | bytes 786440 | tf_op jit(solution)/shard_map/ppermute | solution.py:28
  48.9 8.3 %collective-permute-start.5 = (bf16[128,1024]{0,1:T(8,128)(2,1)S(1)}, bf16[128,1024]{0,1:T(8,128)(2,1)S(1)}, u32[]{:S(2)}, u32[]{:S(2)}) collective-permute-start(bf16[128,1024]{0,1:T(8,128)(2,1)S(1)} %pad_maximum_fusion.1), channel_id=1, source_target_pairs={{0,3},{1,4},{2,5},{3,6},{4,7},{5,8},{6,9},{7,10},{8,11},{9,12},{10... | collective-permute-start | bytes 786440 | tf_op jit(solution)/shard_map/ppermute | solution.py:28
  57.4 3.9 %collective-permute-done.5 = bf16[128,1024]{0,1:T(8,128)(2,1)S(1)} collective-permute-done((bf16[128,1024]{0,1:T(8,128)(2,1)S(1)}, bf16[128,1024]{0,1:T(8,128)(2,1)S(1)}, u32[]{:S(2)}, u32[]{:S(2)}) %collective-permute-start.5) | collective-permute-done | bytes 262176 | tf_op jit(solution)/shard_map/ppermute | solution.py:28
  61.7 1.2 fusion.41
  62.9 6.9 %fusion.42 = (f32[4,5,128]{2,1,0:T(8,128)S(1)}, f32[4,5,128,1152]{2,3,1,0:T(8,128)}) fusion(pred[128,1152]{0,1:T(8,128)(4,1)S(1)} %copy-done.11, bf16[1152,4,128,1]{0,2,3,1:T(8,128)(2,1)S(1)} %bitcast.103, bf16[128,4,5,128]{0,3,2,1:T(8,128)(2,1)S(1)} %bitcast.106), kind=kOutput, calls=%fused_computation.99 | convolution fusion | flops 766772352 | bytes 13789184 | tf_op jit(solution)/shard_map/sub | solution.py:80
  69.8 5.9 %fusion.8 = bf16[4,5,128,1152]{2,3,1,0:T(8,128)(2,1)S(1)} fusion(f32[4,5,128,1152]{2,3,1,0:T(8,128)} %get-tuple-element.51, f32[4,5,128]{2,1,0:T(8,128)S(1)} %get-tuple-element.50), kind=kLoop, calls=%fused_computation.27 | loop fusion | flops 5898240 | bytes 17704960 | tf_op jit(solution)/shard_map/convert_element_type | solution.py:82
  75.7 3.3 fusion.43
  79.0 2.0 copy.114
  81.0 5.2 %fusion.19 = (f32[4,5,128]{2,1,0:T(8,128)S(1)}, bf16[4,128,5,128]{3,1,2,0:T(8,128)(2,1)}) fusion(bf16[4,5,128,128]{2,3,1,0:T(8,128)(2,1)S(1)} %bitcast.99, bf16[1152,4,128,1]{0,2,3,1:T(8,128)(2,1)} %bitcast.101, bf16[4,5,128,1152]{2,3,1,0:T(8,128)(2,1)} %copy-done), kind=kOutput, calls=%fused_computation.40 | convolution fusion | flops 756610560 | bytes 8398848 | tf_op jit(solution)/shard_map/ghij,jgd->ighd/dot_general | solution.py:83
  86.2 5.6 %fusion.3 = bf16[4,5,128,1152]{2,3,1,0:T(8,128)(2,1)S(1)} fusion(bf16[1152,4,128,1]{0,2,3,1:T(8,128)(2,1)S(1)} %bitcast.102, bf16[128,4,5,128]{0,3,2,1:T(8,128)(2,1)S(1)} %bitcast.100, f32[4,5,128]{2,1,0:T(8,128)S(1)} %get-tuple-element.52, f32[4,5,128,1152]{2,3,1,0:T(8,128)} %get-tuple-element.51, f32[4,5,128]{2,1,0:T(8,128)S(1)} %get-tuple-element.50), kind=kOutput, calls=%fused_computation.3 | convolution fusion | flops 766771200 | bytes 19550208 | tf_op jit(solution)/shard_map/ighd,jgd->ghij/dot_general | solution.py:88
  91.9 3.3 fusion.9
  95.1 3.1 copy.113
  98.2 2.0 fusion.30
  100.3 3.8 %collective-permute-start.8 = (f32[128,1024]{1,0:T(8,128)S(1)}, f32[128,1024]{1,0:T(8,128)S(1)}, u32[]{:S(2)}, u32[]{:S(2)}) collective-permute-start(f32[128,1024]{1,0:T(8,128)S(1)} %get-tuple-element.30), channel_id=1, source_target_pairs={{1,0},{2,1},{3,2},{4,3},{5,4},{6,5},{7,6},{8,7},{9,8},{10,9},{11,1... | collective-permute-start | bytes 1572872 | tf_op jit(solution)/shard_map/ppermute | solution.py:28
  104.0 1.9 collective-permute-start.9
  106.0 2.1 collective-permute-start.10
  108.1 1.3 collective-permute-start.11
  109.4 1.3 collective-permute-start.12
  110.7 7.2 %collective-permute-done.8 = f32[128,1024]{1,0:T(8,128)S(1)} collective-permute-done((f32[128,1024]{1,0:T(8,128)S(1)}, f32[128,1024]{1,0:T(8,128)S(1)}, u32[]{:S(2)}, u32[]{:S(2)}) %collective-permute-start.8) | collective-permute-done | bytes 524320 | tf_op jit(solution)/shard_map/ppermute | solution.py:28
  117.9 1.3 collective-permute-start.13
  119.2 17.8 %collective-permute-done.9 = f32[128,1024]{1,0:T(8,128)S(1)} collective-permute-done((f32[128,1024]{1,0:T(8,128)S(1)}, f32[128,1024]{1,0:T(8,128)S(1)}, u32[]{:S(2)}, u32[]{:S(2)}) %collective-permute-start.9) | collective-permute-done | bytes 524320 | tf_op jit(solution)/shard_map/ppermute | solution.py:28
  137.0 1.3 collective-permute-start.15
  138.3 1.3 collective-permute-start.14
  139.6 14.1 %collective-permute-done.11 = f32[128,1024]{1,0:T(8,128)S(1)} collective-permute-done((f32[128,1024]{1,0:T(8,128)S(1)}, f32[128,1024]{1,0:T(8,128)S(1)}, u32[]{:S(2)}, u32[]{:S(2)}) %collective-permute-start.11) | collective-permute-done | bytes 524320 | tf_op jit(solution)/shard_map/ppermute | solution.py:28
  153.7 30.5 %collective-permute-done.12 = f32[128,1024]{1,0:T(8,128)S(1)} collective-permute-done((f32[128,1024]{1,0:T(8,128)S(1)}, f32[128,1024]{1,0:T(8,128)S(1)}, u32[]{:S(2)}, u32[]{:S(2)}) %collective-permute-start.12) | collective-permute-done | bytes 524320 | tf_op jit(solution)/shard_map/ppermute | solution.py:28
  184.2 31.7 %collective-permute-done.13 = f32[128,1024]{1,0:T(8,128)S(1)} collective-permute-done((f32[128,1024]{1,0:T(8,128)S(1)}, f32[128,1024]{1,0:T(8,128)S(1)}, u32[]{:S(2)}, u32[]{:S(2)}) %collective-permute-start.13) | collective-permute-done | bytes 524320 | tf_op jit(solution)/shard_map/ppermute | solution.py:28
  216.5 1.6 stack.2
  218.1 25.0 %all-to-all-start = ((bf16[8,128,1024]{2,1,0:T(8,128)(2,1)}), bf16[8,128,1024]{2,1,0:T(8,128)(2,1)}, u32[]{:S(2)}, u32[]{:S(2)}) async-start(bf16[8,128,1024]{2,1,0:T(8,128)(2,1)} %stack.2), calls=%async_computation | async-start | bytes 4194304 | tf_op jit(solution)/shard_map/all_to_all | solution.py:18
  243.1 0.8 copy.115
  244.4 3.6 constant_dynamic-slice_fusion.1
  248.0 1.2 copy.117
  249.1 1.8 collective-permute-start.16
  250.9 1.8 copy.118
  252.7 1.2 copy.119
  253.9 3.3 collective-permute-start.18
  257.7 3.0 collective-permute-start.20
  261.2 11.0 %collective-permute-done.16 = bf16[128,640]{1,0:T(8,128)(2,1)S(1)} collective-permute-done((bf16[128,640]{1,0:T(8,128)(2,1)S(1)}, bf16[128,640]{1,0:T(8,128)(2,1)S(1)}, u32[]{:S(2)}, u32[]{:S(2)}) %collective-permute-start.16) | collective-permute-done | bytes 163872 | tf_op jit(solution)/shard_map/ppermute | solution.py:54
  272.3 1.2 collective-permute-start.21
  273.4 0.7 constant_dynamic-update-slice_fusion.15
  274.1 2.6 collective-permute-done.17
  276.7 2.6 collective-permute-start.22
  279.3 0.7 constant_dynamic-update-slice_fusion.14
  284.1 5.1 %fusion.15 = f32[640,1024]{1,0:T(8,128)} fusion(bf16[1024,640]{1,0:T(8,128)(2,1)} %bitcast_dynamic-update-slice_fusion, s32[]{:T(128)S(6)} %select_n.81, bf16[1024,1024]{1,0:T(8,128)(2,1)} %bitcast.44), kind=kOutput, calls=%fused_computation.35 | convolution fusion | flops 1347026944 | bytes 6029316 | tf_op jit(solution)/shard_map/dot_general | solution.py:123
  291.1 3.9 %fusion.18 = bf16[4,128,5,128]{3,1,2,0:T(8,128)(2,1)S(1)} fusion(bf16[1152,4,128,1]{0,2,3,1:T(8,128)(2,1)S(1)} %bitcast.104, bf16[4,5,128,1152]{2,3,1,0:T(8,128)(2,1)} %copy-done.1), kind=kOutput, calls=%fused_computation.37 | convolution fusion | flops 755630080 | bytes 7733248 | tf_op jit(solution)/shard_map/ghij,jgd->ighd/dot_general | solution.py:93
  295.1 1.1 copy.126
  296.2 1.1 copy.125
  297.2 39.6 %reduce-scatter.4.cloned.1.call-done = f32[80,1024]{1,0:T(8,128)} async-done(((f32[640,1024]{1,0:T(8,128)}), f32[80,1024]{1,0:T(8,128)}) %reduce-scatter.4.cloned.1.call-update) | async-done | bytes 327696 | tf_op jit(solution)/shard_map/reduce_scatter | solution.py:126
  336.8 11.5 %fusion = f32[24,1024]{1,0:T(8,128)S(1)} fusion(f32[80,1024]{1,0:T(8,128)} %reduce-scatter.4.cloned.1.call-done), kind=kCustom, calls=%all-reduce-scatter | all-reduce-scatter fusion | flops 98305 | bytes 427008
  348.3 1.9 collective-permute-start.23
  350.2 0.7 slice_bitcast_fusion
  350.9 4.4 %collective-permute-done.23 = f32[12,1024]{1,0:T(8,128)S(1)} collective-permute-done((f32[12,1024]{1,0:T(8,128)S(1)}, f32[12,1024]{1,0:T(8,128)S(1)}, u32[]{:S(2)}, u32[]{:S(2)}) %collective-permute-start.23) | collective-permute-done | bytes 49184
  (80 shorter events, 9.4 us)
Async XLA Ops:
  7.2 25.6 %copy-start.10 = (bf16[1,128,2560]{2,1,0:T(8,128)(2,1)S(1)}, bf16[1,128,2560]{2,1,0:T(8,128)(2,1)}, u32[]{:S(2)}) copy-start(bf16[1,128,2560]{2,1,0:T(8,128)(2,1)} %param.6) | copy-start | bytes 1966084
  9.3 52.2 %collective-permute-start.7 = (bf16[128,1024]{0,1:T(8,128)(2,1)S(1)}, bf16[128,1024]{0,1:T(8,128)(2,1)S(1)}, u32[]{:S(2)}, u32[]{:S(2)}) collective-permute-start(bf16[128,1024]{0,1:T(8,128)(2,1)S(1)} %pad_maximum_fusion.1), channel_id=1, source_target_pairs={{0,1},{1,2},{2,3},{3,4},{4,5},{5,6},{6,7},{7,8},{8,9},{9,10},{10,1... | collective-permute-start | bytes 786440 | tf_op jit(solution)/shard_map/ppermute | solution.py:28
  13.1 48.4 %collective-permute-start.6 = (bf16[128,1024]{0,1:T(8,128)(2,1)S(1)}, bf16[128,1024]{0,1:T(8,128)(2,1)S(1)}, u32[]{:S(2)}, u32[]{:S(2)}) collective-permute-start(bf16[128,1024]{0,1:T(8,128)(2,1)S(1)} %pad_maximum_fusion.1), channel_id=1, source_target_pairs={{0,2},{1,3},{2,4},{3,5},{4,6},{5,7},{6,8},{7,9},{8,10},{9,11},{10,... | collective-permute-start | bytes 786440 | tf_op jit(solution)/shard_map/ppermute | solution.py:28
  16.3 32.6 %collective-permute-start.2 = (bf16[128,1024]{0,1:T(8,128)(2,1)S(1)}, bf16[128,1024]{0,1:T(8,128)(2,1)S(1)}, u32[]{:S(2)}, u32[]{:S(2)}) collective-permute-start(bf16[128,1024]{0,1:T(8,128)(2,1)S(1)} %pad_maximum_fusion.1), channel_id=1, source_target_pairs={{0,6},{1,7},{2,8},{3,9},{4,10},{5,11},{6,12},{7,13},{8,14},{9,15},... | collective-permute-start | bytes 786440 | tf_op jit(solution)/shard_map/ppermute | solution.py:28
  20.3 20.4 %collective-permute-start.1 = (bf16[128,1024]{0,1:T(8,128)(2,1)S(1)}, bf16[128,1024]{0,1:T(8,128)(2,1)S(1)}, u32[]{:S(2)}, u32[]{:S(2)}) collective-permute-start(bf16[128,1024]{0,1:T(8,128)(2,1)S(1)} %pad_maximum_fusion.1), channel_id=1, source_target_pairs={{0,7},{1,8},{2,9},{3,10},{4,11},{5,12},{6,13},{7,14},{8,15},{9,16}... | collective-permute-start | bytes 786440 | tf_op jit(solution)/shard_map/ppermute | solution.py:28
  23.8 12.8 %collective-permute-start = (bf16[128,1024]{0,1:T(8,128)(2,1)S(1)}, bf16[128,1024]{0,1:T(8,128)(2,1)}, u32[]{:S(2)}, u32[]{:S(2)}) collective-permute-start(bf16[128,1024]{0,1:T(8,128)(2,1)S(1)} %pad_maximum_fusion.1), channel_id=1, source_target_pairs={{0,8},{1,9},{2,10},{3,11},{4,12},{5,13},{6,14},{7,15},{8,16},{9,17... | collective-permute-start | bytes 786440 | tf_op jit(solution)/shard_map/ppermute | solution.py:28
  33.1 29.9 %copy-start.7 = (bf16[1,128,2560]{1,2,0:T(8,128)(2,1)}, bf16[1,128,2560]{1,2,0:T(8,128)(2,1)S(1)}, u32[]{:S(2)}) copy-start(bf16[1,128,2560]{1,2,0:T(8,128)(2,1)S(1)} %copy.103) | copy-start | bytes 1966084
  36.5 20.8 %collective-permute-start.3 = (bf16[128,1024]{0,1:T(8,128)(2,1)S(1)}, bf16[128,1024]{0,1:T(8,128)(2,1)S(1)}, u32[]{:S(2)}, u32[]{:S(2)}) collective-permute-start(bf16[128,1024]{0,1:T(8,128)(2,1)S(1)} %pad_maximum_fusion.1), channel_id=1, source_target_pairs={{0,5},{1,6},{2,7},{3,8},{4,9},{5,10},{6,11},{7,12},{8,13},{9,14},{... | collective-permute-start | bytes 786440 | tf_op jit(solution)/shard_map/ppermute | solution.py:28
  40.7 16.6 %collective-permute-start.4 = (bf16[128,1024]{0,1:T(8,128)(2,1)S(1)}, bf16[128,1024]{0,1:T(8,128)(2,1)S(1)}, u32[]{:S(2)}, u32[]{:S(2)}) collective-permute-start(bf16[128,1024]{0,1:T(8,128)(2,1)S(1)} %pad_maximum_fusion.1), channel_id=1, source_target_pairs={{0,4},{1,5},{2,6},{3,7},{4,8},{5,9},{6,10},{7,11},{8,12},{9,13},{1... | collective-permute-start | bytes 786440 | tf_op jit(solution)/shard_map/ppermute | solution.py:28
  48.9 12.5 %collective-permute-start.5 = (bf16[128,1024]{0,1:T(8,128)(2,1)S(1)}, bf16[128,1024]{0,1:T(8,128)(2,1)S(1)}, u32[]{:S(2)}, u32[]{:S(2)}) collective-permute-start(bf16[128,1024]{0,1:T(8,128)(2,1)S(1)} %pad_maximum_fusion.1), channel_id=1, source_target_pairs={{0,3},{1,4},{2,5},{3,6},{4,7},{5,8},{6,9},{7,10},{8,11},{9,12},{10... | collective-permute-start | bytes 786440 | tf_op jit(solution)/shard_map/ppermute | solution.py:28
  61.7 1.3 copy-start.11
  62.9 6.9 %copy-start.4 = (bf16[1152,512]{0,1:T(8,128)(2,1)}, bf16[1152,512]{0,1:T(8,128)(2,1)S(1)}, u32[]{:S(2)}) copy-start(bf16[1152,512]{0,1:T(8,128)(2,1)S(1)} %get-tuple-element.38) | copy-start | bytes 3538948
  75.7 3.3 copy-start
  81.0 5.2 %copy-start.3 = (bf16[1152,512]{0,1:T(8,128)(2,1)S(1)}, bf16[1152,512]{0,1:T(8,128)(2,1)}, u32[]{:S(2)}) copy-start(bf16[1152,512]{0,1:T(8,128)(2,1)} %get-tuple-element.39) | copy-start | bytes 3538948
  86.2 5.6 %copy-start.8 = (bf16[1,128,2560]{1,2,0:T(8,128)(2,1)S(1)}, bf16[1,128,2560]{1,2,0:T(8,128)(2,1)}, u32[]{:S(2)}) copy-start(bf16[1,128,2560]{1,2,0:T(8,128)(2,1)} %copy-done.7) | copy-start | bytes 1966084
  91.8 3.3 copy-start.1
  98.2 117.7 %copy-start.2 = (f32[1152,512]{1,0:T(8,128)S(1)}, f32[1152,512]{1,0:T(8,128)}, u32[]{:S(2)}) copy-start(f32[1152,512]{1,0:T(8,128)} %copy.113) | copy-start | bytes 7077892
  100.3 17.6 %collective-permute-start.8 = (f32[128,1024]{1,0:T(8,128)S(1)}, f32[128,1024]{1,0:T(8,128)S(1)}, u32[]{:S(2)}, u32[]{:S(2)}) collective-permute-start(f32[128,1024]{1,0:T(8,128)S(1)} %get-tuple-element.30), channel_id=1, source_target_pairs={{1,0},{2,1},{3,2},{4,3},{5,4},{6,5},{7,6},{8,7},{9,8},{10,9},{11,1... | collective-permute-start | bytes 1572872 | tf_op jit(solution)/shard_map/ppermute | solution.py:28
  104.0 32.9 %collective-permute-start.9 = (f32[128,1024]{1,0:T(8,128)S(1)}, f32[128,1024]{1,0:T(8,128)S(1)}, u32[]{:S(2)}, u32[]{:S(2)}) collective-permute-start(f32[128,1024]{1,0:T(8,128)S(1)} %get-tuple-element.31), channel_id=1, source_target_pairs={{2,0},{3,1},{4,2},{5,3},{6,4},{7,5},{8,6},{9,7},{10,8},{11,9},{12,... | collective-permute-start | bytes 1572872 | tf_op jit(solution)/shard_map/ppermute | solution.py:28
  106.0 32.3 %collective-permute-start.10 = (f32[128,1024]{1,0:T(8,128)S(1)}, f32[128,1024]{1,0:T(8,128)S(1)}, u32[]{:S(2)}, u32[]{:S(2)}) collective-permute-start(f32[128,1024]{1,0:T(8,128)S(1)} %get-tuple-element.32), channel_id=1, source_target_pairs={{3,0},{4,1},{5,2},{6,3},{7,4},{8,5},{9,6},{10,7},{11,8},{12,9},{13... | collective-permute-start | bytes 1572872 | tf_op jit(solution)/shard_map/ppermute | solution.py:28
  108.1 45.6 %collective-permute-start.11 = (f32[128,1024]{1,0:T(8,128)S(1)}, f32[128,1024]{1,0:T(8,128)S(1)}, u32[]{:S(2)}, u32[]{:S(2)}) collective-permute-start(f32[128,1024]{1,0:T(8,128)S(1)} %get-tuple-element.33), channel_id=1, source_target_pairs={{4,0},{5,1},{6,2},{7,3},{8,4},{9,5},{10,6},{11,7},{12,8},{13,9},{1... | collective-permute-start | bytes 1572872 | tf_op jit(solution)/shard_map/ppermute | solution.py:28
  109.4 74.8 %collective-permute-start.12 = (f32[128,1024]{1,0:T(8,128)S(1)}, f32[128,1024]{1,0:T(8,128)S(1)}, u32[]{:S(2)}, u32[]{:S(2)}) collective-permute-start(f32[128,1024]{1,0:T(8,128)S(1)} %get-tuple-element.34), channel_id=1, source_target_pairs={{5,0},{6,1},{7,2},{8,3},{9,4},{10,5},{11,6},{12,7},{13,8},{14,9},{... | collective-permute-start | bytes 1572872 | tf_op jit(solution)/shard_map/ppermute | solution.py:28
  117.9 98.0 %collective-permute-start.13 = (f32[128,1024]{1,0:T(8,128)S(1)}, f32[128,1024]{1,0:T(8,128)S(1)}, u32[]{:S(2)}, u32[]{:S(2)}) collective-permute-start(f32[128,1024]{1,0:T(8,128)S(1)} %get-tuple-element.35), channel_id=1, source_target_pairs={{6,0},{7,1},{8,2},{9,3},{10,4},{11,5},{12,6},{13,7},{14,8},{15,9},... | collective-permute-start | bytes 1572872 | tf_op jit(solution)/shard_map/ppermute | solution.py:28
  137.0 79.0 %collective-permute-start.15 = (f32[128,1024]{1,0:T(8,128)S(1)}, f32[128,1024]{1,0:T(8,128)S(1)}, u32[]{:S(2)}, u32[]{:S(2)}) collective-permute-start(f32[128,1024]{1,0:T(8,128)S(1)} %get-tuple-element.36), channel_id=1, source_target_pairs={{8,0},{9,1},{10,2},{11,3},{12,4},{13,5},{14,6},{15,7},{16,8},{17,9... | collective-permute-start | bytes 1572872 | tf_op jit(solution)/shard_map/ppermute | solution.py:28
  138.3 77.7 %collective-permute-start.14 = (f32[128,1024]{1,0:T(8,128)S(1)}, f32[128,1024]{1,0:T(8,128)S(1)}, u32[]{:S(2)}, u32[]{:S(2)}) collective-permute-start(f32[128,1024]{1,0:T(8,128)S(1)} %get-tuple-element.37), channel_id=1, source_target_pairs={{7,0},{8,1},{9,2},{10,3},{11,4},{12,5},{13,6},{14,7},{15,8},{16,9}... | collective-permute-start | bytes 1572872 | tf_op jit(solution)/shard_map/ppermute | solution.py:28
  218.1 25.0 %copy-start.9 = (bf16[1,128,5120]{2,1,0:T(8,128)(2,1)S(1)}, bf16[1,128,5120]{2,1,0:T(8,128)(2,1)}, u32[]{:S(2)}) copy-start(bf16[1,128,5120]{2,1,0:T(8,128)(2,1)} %param.10) | copy-start | bytes 3932164
  218.1 66.0 %all-to-all-start = ((bf16[8,128,1024]{2,1,0:T(8,128)(2,1)}), bf16[8,128,1024]{2,1,0:T(8,128)(2,1)}, u32[]{:S(2)}, u32[]{:S(2)}) async-start(bf16[8,128,1024]{2,1,0:T(8,128)(2,1)} %stack.2), calls=%async_computation | async-start | bytes 4194304 | tf_op jit(solution)/shard_map/all_to_all | solution.py:18
  243.1 93.7 %reduce-scatter.4.cloned.1.call-start = ((), (), s32[]{:S(2)}) async-start(), calls=%async_computation.2 | async-start | bytes 2949120 | tf_op jit(solution)/shard_map/reduce_scatter | solution.py:126
  249.1 23.1 %collective-permute-start.16 = (bf16[128,640]{1,0:T(8,128)(2,1)S(1)}, bf16[128,640]{1,0:T(8,128)(2,1)S(1)}, u32[]{:S(2)}, u32[]{:S(2)}) collective-permute-start(bf16[128,640]{1,0:T(8,128)(2,1)S(1)} %bitcast.117), channel_id=1, source_target_pairs={{0,7},{1,0},{2,1},{3,2},{4,3},{5,4},{6,5},{7,6},{8,15},{9,8},{10,9... | collective-permute-start | bytes 491528 | tf_op jit(solution)/shard_map/ppermute | solution.py:54
  252.7 23.9 %collective-permute-start.17 = (bf16[128,640]{1,0:T(8,128)(2,1)}, bf16[128,640]{1,0:T(8,128)(2,1)S(1)}, u32[]{:S(2)}, u32[]{:S(2)}) collective-permute-start(bf16[128,640]{1,0:T(8,128)(2,1)} %bitcast.37), channel_id=1, source_target_pairs={{0,6},{1,7},{2,0},{3,1},{4,2},{5,3},{6,4},{7,5},{8,14},{9,15},{10,... | collective-permute-start | bytes 491528 | tf_op jit(solution)/shard_map/ppermute | solution.py:54
  253.9 26.1 %collective-permute-start.18 = (bf16[128,640]{1,0:T(8,128)(2,1)S(1)}, bf16[128,640]{1,0:T(8,128)(2,1)S(1)}, u32[]{:S(2)}, u32[]{:S(2)}) collective-permute-start(bf16[128,640]{1,0:T(8,128)(2,1)S(1)} %bitcast.116), channel_id=1, source_target_pairs={{0,5},{1,6},{2,7},{3,0},{4,1},{5,2},{6,3},{7,4},{8,13},{9,14},{10,... | collective-permute-start | bytes 491528 | tf_op jit(solution)/shard_map/ppermute | solution.py:54
  257.4 23.3 %collective-permute-start.19 = (bf16[128,640]{1,0:T(8,128)(2,1)S(1)}, bf16[128,640]{1,0:T(8,128)(2,1)S(1)}, u32[]{:S(2)}, u32[]{:S(2)}) collective-permute-start(bf16[128,640]{1,0:T(8,128)(2,1)S(1)} %bitcast.114), channel_id=1, source_target_pairs={{0,4},{1,5},{2,6},{3,7},{4,0},{5,1},{6,2},{7,3},{8,12},{9,13},{10,... | collective-permute-start | bytes 491528 | tf_op jit(solution)/shard_map/ppermute | solution.py:54
  257.7 23.7 %collective-permute-start.20 = (bf16[128,640]{1,0:T(8,128)(2,1)S(1)}, bf16[128,640]{1,0:T(8,128)(2,1)S(1)}, u32[]{:S(2)}, u32[]{:S(2)}) collective-permute-start(bf16[128,640]{1,0:T(8,128)(2,1)S(1)} %bitcast.113), channel_id=1, source_target_pairs={{0,3},{1,4},{2,5},{3,6},{4,7},{5,0},{6,1},{7,2},{8,11},{9,12},{10,... | collective-permute-start | bytes 491528 | tf_op jit(solution)/shard_map/ppermute | solution.py:54
  272.3 9.8 %collective-permute-start.21 = (bf16[128,640]{1,0:T(8,128)(2,1)S(1)}, bf16[128,640]{1,0:T(8,128)(2,1)S(1)}, u32[]{:S(2)}, u32[]{:S(2)}) collective-permute-start(bf16[128,640]{1,0:T(8,128)(2,1)S(1)} %bitcast.118), channel_id=1, source_target_pairs={{0,2},{1,3},{2,4},{3,5},{4,6},{5,7},{6,0},{7,1},{8,10},{9,11},{10,... | collective-permute-start | bytes 491528 | tf_op jit(solution)/shard_map/ppermute | solution.py:54
  276.7 6.0 %collective-permute-start.22 = (bf16[128,640]{1,0:T(8,128)(2,1)S(1)}, bf16[128,640]{1,0:T(8,128)(2,1)S(1)}, u32[]{:S(2)}, u32[]{:S(2)}) collective-permute-start(bf16[128,640]{1,0:T(8,128)(2,1)S(1)} %bitcast.115), channel_id=1, source_target_pairs={{0,1},{1,2},{2,3},{3,4},{4,5},{5,6},{6,7},{7,0},{8,9},{9,10},{10,1... | collective-permute-start | bytes 491528 | tf_op jit(solution)/shard_map/ppermute | solution.py:54
  289.2 0.7 copy-start.12
  289.2 1.9 copy-start.5
  291.1 5.0 %copy-start.6 = (bf16[4,128,5,128]{3,1,2,0:T(8,128)(2,1)S(1)}, bf16[4,128,5,128]{3,1,2,0:T(8,128)(2,1)}, u32[]{:S(2)}) copy-start(bf16[4,128,5,128]{3,1,2,0:T(8,128)(2,1)} %get-tuple-element.53) | copy-start | bytes 1966084
  348.3 7.1 %collective-permute-start.23 = (f32[12,1024]{1,0:T(8,128)S(1)}, f32[12,1024]{1,0:T(8,128)S(1)}, u32[]{:S(2)}, u32[]{:S(2)}) collective-permute-start(f32[12,1024]{1,0:T(8,128)S(1)} %slice.72), channel_id=1, source_target_pairs={{0,64},{64,128},{128,192},{1,65},{65,129},{129,193},{2,66},{66,130... | collective-permute-start | bytes 147464
Sparse Core Ops, SparseCore 0:
  289.3 47.4 reduce-scatter.3
